TPU v7x, 32 devices: a whole 2x2x4 slice. The times are simulated.
32 devices in a mesh: seq: 2 (over core), narrow: 4 (over y, x), wide: 4 (over z).
Axes of the slice: x: 2, y: 2, z: 4, core: 2. Of those that a mesh axis runs over, the one named last changes fastest.
Arguments:
- tokens: bfloat16 [8192, 2048], P('seq', 'narrow'), may hold values from -6 to 6
- attn_gain: float32 [2048], P('narrow'), may hold values from 0.5 to 1.5
- w_query: bfloat16 [2048, 2048], P('narrow', 'wide'), may hold values from -0.125 to 0.125
- w_key: bfloat16 [2048, 512], P('narrow', 'wide'), may hold values from -0.125 to 0.125
- w_value: bfloat16 [2048, 512], P('narrow', 'wide'), may hold values from -0.125 to 0.125
- w_out: bfloat16 [2048, 2048], P('wide', 'narrow'), may hold values from -2 to 2
- ffn_gain: float32 [2048], P('narrow'), may hold values from 0.5 to 1.5
- w_gate: bfloat16 [2048, 8192], P('narrow', 'wide'), may hold values from -0.125 to 0.125
- w_up: bfloat16 [2048, 8192], P('narrow', 'wide'), may hold values from -0.125 to 0.125
- w_down: bfloat16 [8192, 2048], P('wide', 'narrow'), may hold values from -0.0625 to 0.0625
- segment_ids: int32 [8192], replicated, may hold values from 0 to 2, as said below
- token_mask: int32 [8192], replicated, may hold values from 0 to 1, as said below
- out_grad: bfloat16 [8192, 2048], P('seq', 'narrow'), may hold values from -6 to 6
Outputs:
- result: bfloat16 [8192, 2048], P('seq', 'narrow')
- input_grad: float32 [8192, 2048], P('seq', 'narrow')
- grad_attn_gain: float32 [2048], P('narrow')
- grad_w_query: float32 [2048, 2048], P('narrow', 'wide')
- grad_w_key: float32 [2048, 512], P('narrow', 'wide')
- grad_w_value: float32 [2048, 512], P('narrow', 'wide')
- grad_w_out: float32 [2048, 2048], P('wide', 'narrow')
- grad_ffn_gain: float32 [2048], P('narrow')
- grad_w_gate: float32 [2048, 8192], P('narrow', 'wide')
- grad_w_up: float32 [2048, 8192], P('narrow', 'wide')
- grad_w_down: float32 [8192, 2048], P('wide', 'narrow')
Inputs may be any that keep to these rules, and one draw needn't show every extreme that they name: `segment_ids`: the pack holds three sequences in order, ids 0, 1, 2, never falling: the first and the last hold 2 to 256 positions each, the middle one all the rest. `token_mask`: padding is the last positions of each sequence: 1 to 255 of the middle one; of the first and the last, one or more and fewer than the sequence's length; the first position of each sequence is a real token.
All inputs are finite; a program needn't handle non-finite values.
Results may differ from a plain program's by a relative error of at most 0.018.
Values may be sent and summed in bfloat16 or wider, within the bound.
A program may use at most 384 MiB of HBM per device.

v0:
```python
import jax
import jax.numpy as jnp
from jax import lax
from jax.sharding import PartitionSpec as P

D = 2048
HD = 64
EPS = 1e-05
THETA = 500000.0
NEG = -1e30


def positions(segment_ids):
    token_index = jnp.arange(segment_ids.shape[0], dtype=jnp.int32)
    seg_first = jnp.concatenate([jnp.ones((1,), dtype=bool), segment_ids[1:] != segment_ids[:-1]])
    seg_start = lax.cummax(jnp.where(seg_first, token_index, jnp.zeros_like(token_index)), axis=0)
    return token_index - seg_start


def rotation(token_pos):
    half_dim = HD // 2
    frequency = THETA ** (-2.0 * jnp.arange(half_dim, dtype=jnp.float32) / HD)
    angles = token_pos.astype(jnp.float32)[:, None] * frequency[None, :]
    cosine_table = jnp.concatenate([jnp.cos(angles), jnp.cos(angles)], axis=1)
    sine_table = jnp.concatenate([jnp.sin(angles), jnp.sin(angles)], axis=1)
    return (cosine_table, sine_table)


def rotate(vectors, cosine_table, sine_table, turn_sign):
    half_dim = HD // 2
    turned = jnp.concatenate([-vectors[..., half_dim:], vectors[..., :half_dim]], axis=-1)
    return vectors * cosine_table[:, None, :] + turn_sign * turned * sine_table[:, None, :]


def narrow_total(values):
    return lax.psum(values, "narrow")


def wide_total(values):
    return lax.psum(values, "wide")


def gather_rows(values):
    return lax.all_gather(values, "narrow", axis=0, tiled=True)


def rms_norm(values):
    squares = narrow_total(jnp.sum(values * values, axis=1))
    row_scale = lax.rsqrt(squares / D + EPS)
    return (values * row_scale[:, None], row_scale)


def norm_back(grad_h, normed, row_scale, gain_vec):
    grad_normed = grad_h * gain_vec[None, :]
    inner_sum = narrow_total(jnp.sum(grad_normed * normed, axis=1))
    grad_input = row_scale[:, None] * (grad_normed - normed * (inner_sum / D)[:, None])
    return (grad_input, jnp.sum(grad_h * normed, axis=0))


def sum_rows(left_side, weight, product_kind):

    def term_rows():
        if product_kind == "flip":
            return lax.dot_general(
                left_side, weight, (((1,), (1,)), ((), ())), preferred_element_type=jnp.float32
            )
        return jnp.dot(left_side, weight, preferred_element_type=jnp.float32)

    return lax.psum_scatter(term_rows(), "narrow", scatter_dimension=0, tiled=True)


def back_rows(grad_rows, weight, inputs):
    shard_piece = lax.all_gather(grad_rows, "narrow", axis=0, tiled=True)
    product = lax.dot_general(
        shard_piece, weight, (((1,), (1,)), ((), ())), preferred_element_type=jnp.float32
    )
    weight_grad = lax.dot_general(
        inputs, shard_piece, (((0,), (0,)), ((), ())), preferred_element_type=jnp.float32
    )
    return (product, weight_grad)


def body(
    tokens,
    attn_gain,
    w_query,
    w_key,
    w_value,
    w_out,
    ffn_gain,
    w_gate,
    w_up,
    w_down,
    segment_ids,
    token_mask,
    out_grad,
):
    narrow_count = lax.axis_size("narrow")
    tok_count = tokens.shape[0]
    quarter = tok_count // narrow_count
    total_tokens = segment_ids.shape[0]
    seq_index = lax.axis_index("seq")
    narrow_index = lax.axis_index("narrow")
    q_width = w_query.shape[1]
    kv_width = w_key.shape[1]
    q_heads = q_width // HD
    kv_heads = kv_width // HD
    group_size = q_heads // kv_heads
    ff_width = w_gate.shape[1]
    score_scale = HD ** (-0.5)
    cosine_all, sine_all = rotation(positions(segment_ids))
    own_first = seq_index * tok_count + narrow_index * quarter
    own_index = own_first + jnp.arange(quarter, dtype=jnp.int32)
    cosine_table = lax.dynamic_slice_in_dim(cosine_all, own_first, quarter, 0)
    sine_table = lax.dynamic_slice_in_dim(sine_all, own_first, quarter, 0)
    own_segment = lax.dynamic_slice_in_dim(segment_ids, own_first, quarter, 0)
    key_index = jnp.arange(total_tokens, dtype=jnp.int32)
    allowed = (
        (own_segment[:, None] == segment_ids[None, :])
        & (key_index[None, :] <= own_index[:, None])
        & (token_mask[None, :] == 1)
    )
    row_valid = lax.dynamic_slice_in_dim(token_mask, seq_index * tok_count, tok_count, 0)
    grad_low = jnp.where(row_valid[:, None] == 1, out_grad, jnp.zeros_like(out_grad))
    grad_float = grad_low.astype(jnp.float32)
    x_float = tokens.astype(jnp.float32)
    normed_one, scale_one = rms_norm(x_float)
    h_one = (normed_one * attn_gain[None, :]).astype(jnp.bfloat16)
    w_qkv = jnp.concatenate([w_query, w_key, w_value], axis=1)
    qkv_lin = sum_rows(h_one, w_qkv, "plain")
    query_rot = rotate(
        qkv_lin[:, :q_width].reshape(quarter, q_heads, HD), cosine_table, sine_table, 1.0
    ).astype(jnp.bfloat16)
    key_rot = rotate(
        qkv_lin[:, q_width : q_width + kv_width].reshape(quarter, kv_heads, HD),
        cosine_table,
        sine_table,
        1.0,
    ).astype(jnp.bfloat16)
    value_low = qkv_lin[:, q_width + kv_width :].astype(jnp.bfloat16)
    kv_local = jnp.concatenate([key_rot.reshape(quarter, kv_width), value_low], axis=1)
    kv_all = lax.all_gather(kv_local, ("seq", "narrow"), axis=0, tiled=True)
    keys_all = kv_all[:, :kv_width].reshape(total_tokens, kv_heads, HD)
    values_all = kv_all[:, kv_width:].reshape(total_tokens, kv_heads, HD)
    query_heads = jnp.transpose(query_rot, (1, 0, 2))
    head_ids = jnp.arange(q_heads, dtype=jnp.int32)

    def head_scores(query_one, head_id):
        kv_id = head_id // group_size
        key_one = lax.dynamic_index_in_dim(keys_all, kv_id, 1, keepdims=False)
        value_one = lax.dynamic_index_in_dim(values_all, kv_id, 1, keepdims=False)
        scores = (
            lax.dot_general(
                query_one, key_one, (((1,), (1,)), ((), ())), preferred_element_type=jnp.float32
            )
            * score_scale
        )
        return (jnp.where(allowed, scores, NEG), key_one, value_one)

    def head_forward(packed):
        query_one, head_id = packed
        scores, key_one, value_one = head_scores(query_one, head_id)
        row_top = jnp.max(scores, axis=1, keepdims=True)
        log_total = row_top + jnp.log(jnp.sum(jnp.exp(scores - row_top), axis=1, keepdims=True))
        prob_low = jnp.exp(scores - log_total).astype(jnp.bfloat16)
        return (jnp.dot(prob_low, value_one, preferred_element_type=jnp.float32), log_total[:, 0])

    head_out, log_totals = lax.map(head_forward, (query_heads, head_ids))
    attn_heads = jnp.transpose(head_out, (1, 0, 2)).reshape(quarter, q_width).astype(jnp.bfloat16)
    attn_all = gather_rows(attn_heads)
    middle = x_float + wide_total(jnp.dot(attn_all, w_out, preferred_element_type=jnp.float32))
    normed_two, scale_two = rms_norm(middle)
    h_two = (normed_two * ffn_gain[None, :]).astype(jnp.bfloat16)
    w_gate_up = jnp.concatenate([w_gate, w_up], axis=1)
    gate_up = sum_rows(h_two, w_gate_up, "plain")
    gate_lin = gate_up[:, :ff_width]
    up_lin = gate_up[:, ff_width:]
    gate_sig = jax.nn.sigmoid(gate_lin)
    act_low = (gate_lin * gate_sig * up_lin).astype(jnp.bfloat16)
    act_all = gather_rows(act_low)
    down_sum = wide_total(jnp.dot(act_all, w_down, preferred_element_type=jnp.float32))
    result = (middle + down_sum).astype(jnp.bfloat16)
    grad_w_down = lax.dot_general(
        act_all, grad_low, (((0,), (0,)), ((), ())), preferred_element_type=jnp.float32
    )
    act_grad = sum_rows(grad_low, w_down, "flip")
    gate_grad = act_grad * up_lin * gate_sig * (1.0 + gate_lin * (1.0 - gate_sig))
    up_grad = act_grad * gate_lin * gate_sig
    gate_up_grad = jnp.concatenate([gate_grad, up_grad], axis=1).astype(jnp.bfloat16)
    middle_part, grad_gate_up = back_rows(gate_up_grad, w_gate_up, h_two)
    middle_norm_grad, grad_ffn_gain = norm_back(
        wide_total(middle_part), normed_two, scale_two, ffn_gain
    )
    middle_grad = grad_float + middle_norm_grad
    attn_grad_low = middle_grad.astype(jnp.bfloat16)
    grad_w_out = lax.dot_general(
        attn_all, attn_grad_low, (((0,), (0,)), ((), ())), preferred_element_type=jnp.float32
    )
    heads_grad = sum_rows(attn_grad_low, w_out, "flip").astype(jnp.bfloat16)
    heads_grad_split = jnp.transpose(heads_grad.reshape(quarter, q_heads, HD), (1, 0, 2))

    def head_backward(packed):
        query_one, grad_one, log_total, head_id = packed
        scores, key_one, value_one = head_scores(query_one, head_id)
        attn_prob = jnp.exp(scores - log_total[:, None])
        prob_low = attn_prob.astype(jnp.bfloat16)
        prob_grad = lax.dot_general(
            grad_one, value_one, (((1,), (1,)), ((), ())), preferred_element_type=jnp.float32
        )
        inner_sum = jnp.sum(attn_prob * prob_grad, axis=1, keepdims=True)
        score_grad = (attn_prob * (prob_grad - inner_sum)).astype(jnp.bfloat16)
        query_grad = jnp.dot(score_grad, key_one, preferred_element_type=jnp.float32) * score_scale
        key_grad = (
            lax.dot_general(
                score_grad, query_one, (((0,), (0,)), ((), ())), preferred_element_type=jnp.float32
            )
            * score_scale
        )
        value_grad = lax.dot_general(
            prob_low, grad_one, (((0,), (0,)), ((), ())), preferred_element_type=jnp.float32
        )
        return (query_grad, key_grad, value_grad)

    query_grads, key_grads, value_grads = lax.map(
        head_backward, (query_heads, heads_grad_split, log_totals, head_ids)
    )
    key_sum = jnp.sum(key_grads.reshape(kv_heads, group_size, total_tokens, HD), axis=1)
    value_sum = jnp.sum(value_grads.reshape(kv_heads, group_size, total_tokens, HD), axis=1)
    kv_grad_all = jnp.concatenate(
        [
            jnp.transpose(key_sum, (1, 0, 2)).reshape(total_tokens, kv_width),
            jnp.transpose(value_sum, (1, 0, 2)).reshape(total_tokens, kv_width),
        ],
        axis=1,
    )
    kv_grad = lax.psum_scatter(
        kv_grad_all.astype(jnp.bfloat16), ("seq", "narrow"), scatter_dimension=0, tiled=True
    ).astype(jnp.float32)
    query_back = rotate(
        jnp.transpose(query_grads, (1, 0, 2)), cosine_table, sine_table, -1.0
    ).reshape(quarter, q_width)
    key_back = rotate(
        kv_grad[:, :kv_width].reshape(quarter, kv_heads, HD), cosine_table, sine_table, -1.0
    ).reshape(quarter, kv_width)
    qkv_grad = jnp.concatenate([query_back, key_back, kv_grad[:, kv_width:]], axis=1).astype(
        jnp.bfloat16
    )
    first_part, grad_qkv = back_rows(qkv_grad, w_qkv, h_one)
    input_part, grad_attn_gain = norm_back(wide_total(first_part), normed_one, scale_one, attn_gain)
    input_grad = middle_grad + input_part
    summed = (
        lax.psum(grad_attn_gain.astype(jnp.bfloat16), "seq").astype(jnp.float32),
        lax.psum(grad_qkv.astype(jnp.bfloat16), "seq").astype(jnp.float32),
        lax.psum(grad_w_out.astype(jnp.bfloat16), "seq").astype(jnp.float32),
        lax.psum(grad_ffn_gain.astype(jnp.bfloat16), "seq").astype(jnp.float32),
        lax.psum(grad_gate_up.astype(jnp.bfloat16), "seq").astype(jnp.float32),
        lax.psum(grad_w_down.astype(jnp.bfloat16), "seq").astype(jnp.float32),
    )
    qkv_total = summed[1]
    gate_up_total = summed[4]
    return (
        result,
        input_grad,
        summed[0],
        qkv_total[:, :q_width],
        qkv_total[:, q_width : q_width + kv_width],
        qkv_total[:, q_width + kv_width :],
        summed[2],
        summed[3],
        gate_up_total[:, :ff_width],
        gate_up_total[:, ff_width:],
        summed[5],
    )


def solution(mesh):
    return jax.shard_map(
        body,
        mesh=mesh,
        in_specs=(
            P("seq", "narrow"),
            P("narrow"),
            P("narrow", "wide"),
            P("narrow", "wide"),
            P("narrow", "wide"),
            P("wide", "narrow"),
            P("narrow"),
            P("narrow", "wide"),
            P("narrow", "wide"),
            P("wide", "narrow"),
            P(),
            P(),
            P("seq", "narrow"),
        ),
        out_specs=(
            P("seq", "narrow"),
            P("seq", "narrow"),
            P("narrow"),
            P("narrow", "wide"),
            P("narrow", "wide"),
            P("narrow", "wide"),
            P("wide", "narrow"),
            P("narrow"),
            P("narrow", "wide"),
            P("narrow", "wide"),
            P("wide", "narrow"),
        ),
        check_vma=False,
    )
```

profile of v0, /device:TPU:0, one launch (start us, length us, event | category | flops | bytes accessed | tf_op | source)
XLA Modules:
  0.0 4983.6 jit_solution(15209267365387991906)
XLA Ops:
  10.5 17.5 psum.98
  51.3 111.1 %reduce-scatter.5.cloned.1.call-done = f32[1024,768]{1,0:T(8,128)} async-done(((f32[4096,768]{1,0:T(8,128)}), f32[1024,768]{1,0:T(8,128)}) %reduce-scatter.5.cloned.1.call-update) | async-done | bytes 3145744 | tf_op jit(solution)/shard_map/reduce_scatter | solution.py:69
  182.3 22.7 all-gather.6.cloned.1.call-done
  217.7 410.5 %while.34 = (s32[]{:T(128)}, bf16[8,1024,64]{1,2,0:T(8,128)(2,1)S(1)}, f32[8,1024]{1,0:T(8,128)}, bf16[8,1024,64]{2,1,0:T(8,128)(2,1)}, s32[8]{0:T(128)S(1)}, /*...) while((s32[]{:T(128)}, ...), condition=%wide.region_8.9_spmd.clone.clone, body=%wide.region_5.8_spmd.clone.sunk.clone | while | flops 2239757312 | bytes 111760208 | solution.py:168
  220.9 19.6 fusion.142
  272.2 19.6 fusion.142
  323.5 19.6 fusion.142
  374.8 19.6 fusion.142
  426.1 19.6 fusion.142
  477.4 19.6 fusion.142
  528.7 19.6 fusion.142
  580.0 19.6 fusion.142
  629.6 52.4 %all-gather.8.cloned.1.call-done = bf16[4096,512]{0,1:T(8,128)(2,1)} async-done(((bf16[1024,512]{0,1:T(8,128)(2,1)}), bf16[4096,512]{0,1:T(8,128)(2,1)}) %all-gather.8.cloned.1.call-update) | async-done | bytes 4194320 | tf_op jit(solution)/shard_map/all_gather | solution.py:44
  690.3 17.7 fusion.82
  714.4 266.7 %all-reduce.10.cloned.1.call-done = f32[4096,512]{1,0:T(8,128)} async-done(((f32[4096,512]{1,0:T(8,128)}), f32[4096,512]{1,0:T(8,128)}) %all-reduce.10.cloned.1.call-update) | async-done | bytes 8388624 | tf_op jit(solution)/shard_map/psum | solution.py:40
  990.3 16.6 psum.100
  1006.9 34.1 fusion.83
  1042.9 229.3 %reduce-scatter.7.cloned.1.call-done = f32[1024,2048]{1,0:T(8,128)} async-done(((f32[4096,2048]{1,0:T(8,128)}), f32[1024,2048]{1,0:T(8,128)}) %reduce-scatter.7.cloned.1.call-update) | async-done | bytes 8388624 | tf_op jit(solution)/shard_map/reduce_scatter | solution.py:69
  1272.2 1120.8 %all-reduce.14.cloned.1.call-done = f32[4096,4096]{1,0:T(8,128)} async-done(((f32[4096,4096]{1,0:T(8,128)}), f32[4096,4096]{1,0:T(8,128)}) %all-reduce.14.cloned.1.call-update) | async-done | bytes 67108880
  2415.0 298.5 %all-gather.12.cloned.1.call-done = bf16[4096,4096]{1,0:T(8,128)(2,1)} async-done(((bf16[1024,4096]{1,0:T(8,128)(2,1)}), bf16[4096,4096]{1,0:T(8,128)(2,1)}) %all-gather.12.cloned.1.call-update) | async-done | bytes 33554448 | tf_op jit(solution)/shard_map/all_gather | solution.py:73
  2713.5 25.0 fusion.91
  2738.6 290.9 %all-reduce.12.cloned.1.call-done = f32[4096,512]{1,0:T(8,128)} async-done(((f32[4096,512]{1,0:T(8,128)}), f32[4096,512]{1,0:T(8,128)}) %all-reduce.12.cloned.1.call-update) | async-done | bytes 8388624 | tf_op jit(solution)/shard_map/psum | solution.py:40
  3037.0 16.0 psum.103
  3071.1 83.6 %reduce-scatter.9.cloned.1.call-done = f32[1024,512]{1,0:T(8,128)} async-done(((f32[4096,512]{1,0:T(8,128)}), f32[1024,512]{1,0:T(8,128)}) %reduce-scatter.9.cloned.1.call-update) | async-done | bytes 2097168 | tf_op jit(solution)/shard_map/reduce_scatter | solution.py:69
  3159.0 861.1 %while.35 = (s32[]{:T(128)}, f32[8,1024,64]{1,2,0:T(8,128)}, f32[8,8192,64]{1,2,0:T(8,128)}, f32[8,8192,64]{1,2,0:T(8,128)}, bf16[8,1024,64]{2,1,0:T(8,128)(2,1)...) while((s32[]{:T(128)}, f32[8,1024,64]{1,2,0:T(8,128)}, ...), condition=%wide.region_21.22_spmd.clone.clone, body=%wide.region_19.21_spmd.clone.sunk.clone | while | flops 5478349824 | bytes 344006528 | solution.py:224
  3162.7 14.6 fusion.152
  3178.0 28.8 multiply_reduce_fusion.6
  3206.8 27.5 multiply_convert_fusion.9
  3252.1 14.9 fusion.155
  3270.2 14.6 fusion.152
  3285.6 28.7 multiply_reduce_fusion.6
  3314.3 27.5 multiply_convert_fusion.9
  3359.7 14.9 fusion.155
  3377.8 14.6 fusion.152
  3393.1 28.7 multiply_reduce_fusion.6
  3421.8 27.5 multiply_convert_fusion.9
  3467.2 14.9 fusion.155
  3485.3 14.6 fusion.152
  3500.6 28.7 multiply_reduce_fusion.6
  3529.4 27.5 multiply_convert_fusion.9
  3574.7 15.0 fusion.155
  3592.9 14.6 fusion.152
  3608.2 28.7 multiply_reduce_fusion.6
  3637.0 27.5 multiply_convert_fusion.9
  3682.3 14.9 fusion.155
  3700.4 14.6 fusion.152
  3715.8 28.7 multiply_reduce_fusion.6
  3744.5 27.5 multiply_convert_fusion.9
  3789.9 14.9 fusion.155
  3808.0 14.6 fusion.152
  3823.3 28.7 multiply_reduce_fusion.6
  3852.1 27.5 multiply_convert_fusion.9
  3897.4 14.9 fusion.155
  3930.9 28.7 multiply_reduce_fusion.6
  3959.7 27.5 multiply_convert_fusion.9
  4005.0 14.9 fusion.155
  4039.5 46.7 reduce-scatter.11.cloned.1.call-done
  4090.9 155.2 %all-gather.10.cloned.1.call-done = bf16[4096,2048]{1,0:T(8,128)(2,1)} async-done(((bf16[1024,2048]{1,0:T(8,128)(2,1)}), bf16[4096,2048]{1,0:T(8,128)(2,1)}) %all-gather.10.cloned.1.call-update) | async-done | bytes 16777232 | tf_op jit(solution)/shard_map/all_gather | solution.py:44
  4246.1 14.8 convolution_convert_fusion.1
  4261.0 25.4 convolution_convert_fusion
  4289.5 29.1 all-gather.14.cloned.1.call-done
  4327.7 14.7 fusion.90
  4375.6 554.8 %all-reduce.16.cloned.1.call-done = (f32[4096,512]{1,0:T(8,128)}, f32[4096,512]{1,0:T(8,128)}) async-done(((f32[4096,512]{1,0:T(8,128)}, f32[4096,512]{1,0:T(8,128)}), (f32[4096,512]{1,0:T(8,128)}, f32[4096,512]{1,0:T(8,128)})) %all-reduce.16.cloned.1.call-update) | async-done | bytes 16777232 | tf_op jit(solution)/shard_map/psum | solution.py:40
  4939.9 16.0 psum.105
  (319 shorter events, 638.2 us)
Async XLA Ops:
  7.2 683.1 %copy-start = (bf16[2048,512]{1,0:T(8,128)(2,1)S(1)}, bf16[2048,512]{1,0:T(8,128)(2,1)}, u32[]{:S(2)}) copy-start(bf16[2048,512]{1,0:T(8,128)(2,1)} %param.26) | copy-start | bytes 6291460
  7.2 155.2 %reduce-scatter.5.cloned.1.call-start = ((), (), s32[]{:S(2)}) async-start(), calls=%async_computation.4 | async-start | bytes 15728640 | tf_op jit(solution)/shard_map/reduce_scatter | solution.py:69
  42.1 162.9 %all-gather.6.cloned.1.call-start = ((), (), s32[]{:S(2)}) async-start(), calls=%async_computation.5 | async-start | bytes 4718592 | tf_op jit(solution)/shard_map/all_gather | solution.py:142
  43.7 124.9 %copy-start.21 = (s32[8192]{0:T(1024)S(1)}, s32[8192]{0:T(1024)}, u32[]{:S(2)}) copy-start(s32[8192]{0:T(1024)} %param.28) | copy-start | bytes 98308
  47.4 129.0 %copy-start.7 = (f32[1024,64]{0,1:T(8,128)}, f32[1024,64]{0,1:T(8,128)S(1)}, u32[]{:S(2)}) copy-start(f32[1024,64]{0,1:T(8,128)S(1)} %fusion.80) | copy-start | bytes 786436
  168.2 513.9 %all-gather.8.cloned.1.call-start = ((), (), s32[]{:S(2)}) async-start(), calls=%async_computation.6 | async-start | bytes 5242880 | tf_op jit(solution)/shard_map/all_gather | solution.py:44
  240.4 13.8 copy-start.3
  291.7 13.8 copy-start.3
  343.0 13.8 copy-start.3
  394.4 13.8 copy-start.3
  445.7 13.8 copy-start.3
  497.0 13.8 copy-start.3
  548.3 13.8 copy-start.3
  599.6 13.8 copy-start.3
  628.2 62.0 %copy-start.27 = (pred[8192]{0:T(1024)(128)(4,1)}, pred[8192]{0:T(1024)(128)(4,1)S(1)}, u32[]{:S(2)}) copy-start(pred[8192]{0:T(1024)(128)(4,1)S(1)} %get-tuple-element.864) | copy-start | bytes 24580
  628.2 62.0 %copy-start.31 = (s32[1024]{0:T(1024)}, s32[1024]{0:T(1024)S(1)}, u32[]{:S(2)}) copy-start(s32[1024]{0:T(1024)S(1)} %get-tuple-element.865) | copy-start | bytes 12292
  628.2 62.0 %copy-start.33 = (s32[1024]{0:T(1024)}, s32[1024]{0:T(1024)S(1)}, u32[]{:S(2)}) copy-start(s32[1024]{0:T(1024)S(1)} %get-tuple-element.866) | copy-start | bytes 12292
  629.1 61.1 %copy-start.22 = (s32[8192]{0:T(1024)S(1)}, s32[8192]{0:T(1024)}, u32[]{:S(2)}) copy-start(s32[8192]{0:T(1024)} %param.28) | copy-start | bytes 98308
  629.2 351.9 %all-reduce.10.cloned.1.call-start = ((), (), s32[]{:S(2)}) async-start(), calls=%async_computation.7 | async-start | bytes 16777216 | tf_op jit(solution)/shard_map/psum | solution.py:40
  690.2 582.0 %reduce-scatter.7.cloned.1.call-start = ((), (), s32[]{:S(2)}) async-start(), calls=%async_computation.9 | async-start | bytes 41943040 | tf_op jit(solution)/shard_map/reduce_scatter | solution.py:69
  690.2 2362.8 %copy-start.23 = (pred[4096]{0:T(1024)(128)(4,1)}, pred[4096]{0:T(1024)(128)(4,1)S(1)}, u32[]{:S(2)}) copy-start(pred[4096]{0:T(1024)(128)(4,1)S(1)} %dynamic-slice_compare_fusion) | copy-start | bytes 12292
  708.0 1684.9 %all-reduce.14.cloned.1.call-start = ((), (), s32[]{:S(2)}) async-start(), calls=%async_computation.15 | async-start | bytes 134217728
  714.4 292.4 %copy-start.25 = (f32[512]{0:T(512)S(1)}, f32[512]{0:T(512)}, u32[]{:S(2)}) copy-start(f32[512]{0:T(512)} %param.23) | copy-start | bytes 6148
  1006.9 2046.2 %copy-start.19 = (f32[4096]{0:T(1024)}, f32[4096]{0:T(1024)S(1)}, u32[]{:S(2)}) copy-start(f32[4096]{0:T(1024)S(1)} %add_rsqrt_fusion) | copy-start | bytes 49156
  1041.0 1672.5 %all-gather.12.cloned.1.call-start = ((), (), s32[]{:S(2)}) async-start(), calls=%async_computation.10 | async-start | bytes 41943040 | tf_op jit(solution)/shard_map/all_gather | solution.py:73
  2414.8 614.8 %all-reduce.12.cloned.1.call-start = ((), (), s32[]{:S(2)}) async-start(), calls=%async_computation.11 | async-start | bytes 16777216 | tf_op jit(solution)/shard_map/psum | solution.py:40
  2738.6 416.2 %reduce-scatter.9.cloned.1.call-start = ((), (), s32[]{:S(2)}) async-start(), calls=%async_computation.12 | async-start | bytes 10485760 | tf_op jit(solution)/shard_map/reduce_scatter | solution.py:69
  3053.1 12.1 copy-start.12
  3071.0 88.0 %copy-start.16 = (s32[8192]{0:T(1024)S(1)}, s32[8192]{0:T(1024)}, u32[]{:S(2)}) copy-start(s32[8192]{0:T(1024)} %param.27) | copy-start | bytes 98308
  3071.0 88.0 %copy-start.28 = (pred[8192]{0:T(1024)(128)(4,1)S(1)}, pred[8192]{0:T(1024)(128)(4,1)}, u32[]{:S(2)}) copy-start(pred[8192]{0:T(1024)(128)(4,1)} %copy-done.27) | copy-start | bytes 24580
  3071.0 88.0 %copy-start.32 = (s32[1024]{0:T(1024)S(1)}, s32[1024]{0:T(1024)}, u32[]{:S(2)}) copy-start(s32[1024]{0:T(1024)} %copy-done.31) | copy-start | bytes 12292
  3071.0 88.0 %copy-start.34 = (s32[1024]{0:T(1024)S(1)}, s32[1024]{0:T(1024)}, u32[]{:S(2)}) copy-start(s32[1024]{0:T(1024)} %copy-done.33) | copy-start | bytes 12292
  3071.0 1015.2 %reduce-scatter.11.cloned.1.call-start = ((), (), s32[]{:S(2)}) async-start(), calls=%async_computation.13 | async-start | bytes 4718592 | tf_op jit(solution)/shard_map/reduce_scatter | solution.py:236
  3162.7 15.4 copy-start.4
  3234.3 11.4 copy-start.1
  3234.3 12.0 copy-start.5
  3270.2 15.4 copy-start.4
  3341.8 12.0 copy-start.5
  3377.7 15.4 copy-start.4
  3449.3 12.0 copy-start.5
  3485.3 15.4 copy-start.4
  3556.9 12.0 copy-start.5
  3592.9 15.4 copy-start.4
  3664.5 12.0 copy-start.5
  3700.4 15.4 copy-start.4
  3772.0 12.0 copy-start.5
  3808.0 15.4 copy-start.4
  3879.6 12.0 copy-start.5
  3915.6 15.4 copy-start.4
  3987.2 12.0 copy-start.5
  4034.8 211.3 %all-gather.10.cloned.1.call-start = ((), (), s32[]{:S(2)}) async-start(), calls=%async_computation.8 | async-start | bytes 20971520 | tf_op jit(solution)/shard_map/all_gather | solution.py:44
  4035.5 283.1 %all-gather.14.cloned.1.call-start = ((), (), s32[]{:S(2)}) async-start(), calls=%async_computation.14 | async-start | bytes 7864320 | tf_op jit(solution)/shard_map/all_gather | solution.py:73
  4037.3 208.8 %copy-start.24 = (pred[4096]{0:T(1024)(128)(4,1)S(1)}, pred[4096]{0:T(1024)(128)(4,1)}, u32[]{:S(2)}) copy-start(pred[4096]{0:T(1024)(128)(4,1)} %copy-done.23) | copy-start | bytes 12292
  4090.8 170.2 %copy-start.20 = (f32[4096]{0:T(1024)S(1)}, f32[4096]{0:T(1024)}, u32[]{:S(2)}) copy-start(f32[4096]{0:T(1024)} %copy-done.19) | copy-start | bytes 49156
  4090.8 170.2 %copy-start.26 = (f32[512]{0:T(512)S(1)}, f32[512]{0:T(512)}, u32[]{:S(2)}) copy-start(f32[512]{0:T(512)} %param.23) | copy-start | bytes 6148
  4090.8 271.9 %all-reduce.18.cloned.1.call-start = ((), (), s32[]{:S(2)}) async-start(), calls=%async_computation.17 | async-start | bytes 15204352 | tf_op jit(solution)/shard_map/psum | solution.py:253
  4246.1 40.2 slice-start
  4261.0 25.4 slice-start.1
  4261.0 25.4 copy-start.9
  4286.4 32.2 copy-start.18
  4286.4 32.2 copy-start.29
  4327.7 14.7 copy-start.14
  4327.7 602.7 %all-reduce.16.cloned.1.call-start = ((), (), s32[]{:S(2)}) async-start(), calls=%async_computation.16 | async-start | bytes 33554432 | tf_op jit(solution)/shard_map/psum | solution.py:40
  4375.6 560.7 %copy-start.30 = (bf16[512]{0:T(512)(128)(2,1)S(1)}, bf16[512]{0:T(512)(128)(2,1)}, u32[]{:S(2)}) copy-start(bf16[512]{0:T(512)(128)(2,1)} %get-tuple-element.396) | copy-start | bytes 3076
  (16 other events, 106.6 us)
Sparse Core Ops, SparseCore 0:
  42.2 120.1 reduce-scatter.4
  168.3 36.6 all-gather.5
  629.3 52.7 all-gather.7
  690.2 290.8 all-reduce.9
  984.0 288.1 reduce-scatter.6
  1275.9 1116.9 all-reduce.13
  2414.9 298.5 all-gather.11
  2738.7 290.8 all-reduce.11
  3071.1 83.5 reduce-scatter.8
  4034.9 51.2 reduce-scatter.10
  4088.7 157.4 all-gather.9
  4248.4 70.1 all-gather.13
  4327.8 34.8 all-reduce.17
  4366.0 564.4 all-reduce.15
where the time goes:
time: 4990 us; the launch traced here: 4980 us
  waiting for transfers between devices  3270 us (66%)
  matrix products  1040 us (21%)
  other arithmetic  454 us (9%)
  local copies, waits for them, and re-layouts  90.9 us (2%)
  blocking collectives  68.5 us (1%)
    unnamed x15, waiting for transfers between devices  1120 us
    psum x3, waiting for transfers between devices, wide_total(): return lax.psum(values, 'wide')  1110 us
    reduce_scatter x3, waiting for transfers between devices, sum_rows(): lax.psum_scatter(term_rows(), 'narrow', scatter_dimension=0, tiled=True)  424 us
    dot_general x16, matrix products, head_scores(): lax.dot_general(query_one, key_one, (((1,), (1,)), ((), ())), preferred_e...  386 us
    all_gather x2, waiting for transfers between devices, back_rows(): shard_piece = lax.all_gather(grad_rows, 'narrow', axis=0, tiled=True)  328 us
    convert_element_type x8, other arithmetic, head_backward(): score_grad = (attn_prob * (prob_grad - inner_sum)).astype(jnp.bfloat16)  220 us
    all_gather x2, waiting for transfers between devices, gather_rows(): return lax.all_gather(values, 'narrow', axis=0, tiled=True)  208 us
    dot_general x8, matrix products, head_backward(): lax.dot_general(prob_low, grad_one, (((0,), (0,)), ((), ())), preferred_e...  119 us
  transfers between devices with their start and end apart: 14, of which 14 were waited for; matrix products, arithmetic and copies ran while one was open for 4% of the time, Pallas kernels for 0%

commit v1 on v0

--- a/solution.py
+++ b/solution.py
@@ -37,7 +37,7 @@
 
 
 def wide_total(values):
-    return lax.psum(values, "wide")
+    return jnp.sum(lax.all_gather(values, "wide"), axis=0)
 
 
 def gather_rows(values):

time: 4990 us -> 6080 us (1.22)
  waiting for transfers between devices: 3270 us -> 4290 us
  other arithmetic: 454 us -> 520 us
    all_gather x0 -> x4, waiting for transfers between devices: none -> 2160 us  [wide_total(): return jnp.sum(lax.all_gather(values, 'wide'), axis=0)]
    psum x3 -> x0, waiting for transfers between devices: 1110 us -> none  [wide_total(): return lax.psum(values, 'wide')]
    reduce_sum x0 -> x4, other arithmetic: none -> 71.7 us  [wide_total(): return jnp.sum(lax.all_gather(values, 'wide'), axis=0)]
    unnamed x15 -> x16, waiting for transfers between devices: 1120 us -> 1120 us
  transfers between devices with their start and end apart: 14 -> 15, of which waited for: 14 -> 15; matrix products, arithmetic and copies ran while one was open for 4% -> 4% of each run, Pallas kernels for 0% -> 0%
where the time goes in v1:
time: 6080 us; the launch traced here: 6070 us
  waiting for transfers between devices  4290 us (71%)
  matrix products  1030 us (17%)
  other arithmetic  520 us (9%)
  local copies, waits for them, and re-layouts  94.2 us (2%)
  blocking collectives  68.8 us (1%)
    all_gather x4, waiting for transfers between devices, wide_total(): return jnp.sum(lax.all_gather(values, 'wide'), axis=0)  2160 us
    unnamed x16, waiting for transfers between devices  1120 us
    reduce_scatter x3, waiting for transfers between devices, sum_rows(): lax.psum_scatter(term_rows(), 'narrow', scatter_dimension=0, tiled=True)  404 us
    dot_general x16, matrix products, head_scores(): lax.dot_general(query_one, key_one, (((1,), (1,)), ((), ())), preferred_e...  387 us
    all_gather x2, waiting for transfers between devices, back_rows(): shard_piece = lax.all_gather(grad_rows, 'narrow', axis=0, tiled=True)  310 us
    convert_element_type x8, other arithmetic, head_backward(): score_grad = (attn_prob * (prob_grad - inner_sum)).astype(jnp.bfloat16)  220 us
    all_gather x2, waiting for transfers between devices, gather_rows(): return lax.all_gather(values, 'narrow', axis=0, tiled=True)  203 us
  transfers between devices with their start and end apart: 15, of which 15 were waited for; matrix products, arithmetic and copies ran while one was open for 4% of the time, Pallas kernels for 0%

profile of v1, /device:TPU:0, one launch (start us, length us, event | category | flops | bytes accessed | tf_op | source)
XLA Modules:
  0.0 6068.2 jit_solution(7312360640050126742)
XLA Ops:
  10.5 17.5 psum.70
  51.3 111.1 %reduce-scatter.5.cloned.1.call-done = f32[1024,768]{1,0:T(8,128)} async-done(((f32[4096,768]{1,0:T(8,128)}), f32[1024,768]{1,0:T(8,128)}) %reduce-scatter.5.cloned.1.call-update) | async-done | bytes 3145744 | tf_op jit(solution)/shard_map/reduce_scatter | solution.py:69
  182.5 22.5 all-gather.14.cloned.1.call-done
  217.7 410.7 %while.34 = (s32[]{:T(128)}, bf16[8,1024,64]{1,2,0:T(8,128)(2,1)S(1)}, f32[8,1024]{1,0:T(8,128)}, bf16[8,1024,64]{2,1,0:T(8,128)(2,1)}, s32[8]{0:T(128)S(1)}, /*...) while((s32[]{:T(128)}, ...), condition=%wide.region_8.9_spmd.clone.clone, body=%wide.region_5.8_spmd.clone.sunk.clone | while | flops 2239757312 | bytes 111760208 | solution.py:168
  220.8 19.6 fusion.142
  272.2 19.6 fusion.142
  323.5 19.6 fusion.142
  374.8 19.6 fusion.142
  426.2 19.6 fusion.142
  477.5 19.6 fusion.142
  528.8 19.6 fusion.142
  580.2 19.6 fusion.142
  629.5 52.6 all-gather.16.cloned.1.call-done
  691.0 23.5 fusion.82
  721.2 530.6 %all-gather.24.cloned.1.call-done = f32[16384,512]{1,0:T(8,128)} async-done(((f32[4096,512]{1,0:T(8,128)}), f32[16384,512]{1,0:T(8,128)}) %all-gather.24.cloned.1.call-update) | async-done | bytes 33554448 | tf_op jit(solution)/shard_map/all_gather | solution.py:40
  1251.8 17.3 reduce_sum.133
  1278.5 16.9 psum.71
  1295.4 34.2 fusion.83
  1331.6 210.5 %reduce-scatter.7.cloned.1.call-done = f32[1024,2048]{1,0:T(8,128)} async-done(((f32[4096,2048]{1,0:T(8,128)}), f32[1024,2048]{1,0:T(8,128)}) %reduce-scatter.7.cloned.1.call-update) | async-done | bytes 8388624 | tf_op jit(solution)/shard_map/reduce_scatter | solution.py:69
  1542.1 1120.8 %all-reduce.6.cloned.1.call-done = f32[4096,4096]{1,0:T(8,128)} async-done(((f32[4096,4096]{1,0:T(8,128)}), f32[4096,4096]{1,0:T(8,128)}) %all-reduce.6.cloned.1.call-update) | async-done | bytes 67108880
  2662.8 13.8 multiply_convert_fusion.2
  2685.2 150.5 %all-gather.18.cloned.1.call-done = bf16[4096,2048]{1,0:T(8,128)(2,1)} async-done(((bf16[1024,2048]{1,0:T(8,128)(2,1)}), bf16[4096,2048]{1,0:T(8,128)(2,1)}) %all-gather.18.cloned.1.call-update) | async-done | bytes 16777232 | tf_op jit(solution)/shard_map/all_gather | solution.py:44
  2835.7 15.2 fusion.90
  2850.9 283.8 %all-gather.20.cloned.1.call-done = bf16[4096,4096]{1,0:T(8,128)(2,1)} async-done(((bf16[1024,4096]{1,0:T(8,128)(2,1)}), bf16[4096,4096]{1,0:T(8,128)(2,1)}) %all-gather.20.cloned.1.call-update) | async-done | bytes 33554448 | tf_op jit(solution)/shard_map/all_gather | solution.py:73
  3134.7 27.1 fusion.91
  3161.9 535.8 %all-gather.26.cloned.1.call-done = f32[16384,512]{1,0:T(8,128)} async-done(((f32[4096,512]{1,0:T(8,128)}), f32[16384,512]{1,0:T(8,128)}) %all-gather.26.cloned.1.call-update) | async-done | bytes 33554448 | tf_op jit(solution)/shard_map/all_gather | solution.py:40
  3697.7 20.6 reduce_sum.135
  3718.4 540.4 %all-gather.28.cloned.1.call-done = f32[16384,512]{1,0:T(8,128)} async-done(((f32[4096,512]{1,0:T(8,128)}), f32[16384,512]{1,0:T(8,128)}) %all-gather.28.cloned.1.call-update) | async-done | bytes 33554448 | tf_op jit(solution)/shard_map/all_gather | solution.py:40
  4258.8 16.8 reduce_sum.136
  4283.1 16.0 psum.72
  4320.6 82.9 %reduce-scatter.9.cloned.1.call-done = f32[1024,512]{1,0:T(8,128)} async-done(((f32[4096,512]{1,0:T(8,128)}), f32[1024,512]{1,0:T(8,128)}) %reduce-scatter.9.cloned.1.call-update) | async-done | bytes 2097168 | tf_op jit(solution)/shard_map/reduce_scatter | solution.py:69
  4407.7 849.8 %while.35 = (s32[]{:T(128)}, f32[8,1024,64]{1,2,0:T(8,128)}, f32[8,8192,64]{1,2,0:T(8,128)}, f32[8,8192,64]{1,2,0:T(8,128)}, bf16[8,1024,64]{2,1,0:T(8,128)(2,1)...) while((s32[]{:T(128)}, f32[8,1024,64]{1,2,0:T(8,128)}, ...), condition=%wide.region_21.22_spmd.clone.clone, body=%wide.region_19.21_spmd.clone.sunk.clone | while | flops 5478349824 | bytes 344006080 | solution.py:224
  4425.1 28.7 multiply_reduce_fusion.6
  4453.8 27.5 multiply_convert_fusion.9
  4499.2 14.9 fusion.155
  4531.2 28.7 multiply_reduce_fusion.6
  4560.0 27.5 multiply_convert_fusion.9
  4605.3 14.9 fusion.155
  4637.3 28.7 multiply_reduce_fusion.6
  4666.1 27.5 multiply_convert_fusion.9
  4711.4 14.9 fusion.155
  4743.5 28.7 multiply_reduce_fusion.6
  4772.2 27.5 multiply_convert_fusion.9
  4817.6 14.9 fusion.155
  4849.7 28.7 multiply_reduce_fusion.6
  4878.4 27.5 multiply_convert_fusion.9
  4923.8 15.0 fusion.155
  4955.9 28.7 multiply_reduce_fusion.6
  4984.6 27.5 multiply_convert_fusion.9
  5030.0 14.9 fusion.155
  5062.0 28.7 multiply_reduce_fusion.6
  5090.8 27.5 multiply_convert_fusion.9
  5136.1 14.9 fusion.155
  5168.1 28.7 multiply_reduce_fusion.6
  5196.9 27.5 multiply_convert_fusion.9
  5242.2 14.9 fusion.155
  5276.0 47.7 reduce-scatter.11.cloned.1.call-done
  5328.4 14.8 convolution_convert_fusion.1
  5343.3 25.5 convolution_convert_fusion
  5372.0 26.6 all-gather.22.cloned.1.call-done
  5416.9 25.9 all-reduce.8.cloned.1.call-done
  5457.6 549.8 %all-gather.30.cloned.1.call-done = f32[16384,512]{1,0:T(8,128)} async-done(((f32[4096,512]{1,0:T(8,128)}), f32[16384,512]{1,0:T(8,128)}) %all-gather.30.cloned.1.call-update) | async-done | bytes 33554448 | tf_op jit(solution)/shard_map/all_gather | solution.py:40
  6007.4 16.9 reduce_sum.140
  6033.8 16.0 psum.73
  (333 shorter events, 700.8 us)
Async XLA Ops:
  7.2 683.8 %copy-start = (bf16[2048,512]{1,0:T(8,128)(2,1)S(1)}, bf16[2048,512]{1,0:T(8,128)(2,1)}, u32[]{:S(2)}) copy-start(bf16[2048,512]{1,0:T(8,128)(2,1)} %param.26) | copy-start | bytes 6291460
  7.2 155.2 %reduce-scatter.5.cloned.1.call-start = ((), (), s32[]{:S(2)}) async-start(), calls=%async_computation.4 | async-start | bytes 15728640 | tf_op jit(solution)/shard_map/reduce_scatter | solution.py:69
  42.1 162.9 %all-gather.14.cloned.1.call-start = ((), (), s32[]{:S(2)}) async-start(), calls=%async_computation.5 | async-start | bytes 4718592 | tf_op jit(solution)/shard_map/all_gather | solution.py:142
  43.7 125.2 %copy-start.24 = (s32[8192]{0:T(1024)S(1)}, s32[8192]{0:T(1024)}, u32[]{:S(2)}) copy-start(s32[8192]{0:T(1024)} %param.28) | copy-start | bytes 98308
  47.4 129.3 %copy-start.10 = (f32[1024,64]{0,1:T(8,128)}, f32[1024,64]{0,1:T(8,128)S(1)}, u32[]{:S(2)}) copy-start(f32[1024,64]{0,1:T(8,128)S(1)} %fusion.80) | copy-start | bytes 786436
  168.1 514.0 %all-gather.16.cloned.1.call-start = ((), (), s32[]{:S(2)}) async-start(), calls=%async_computation.6 | async-start | bytes 5242880 | tf_op jit(solution)/shard_map/all_gather | solution.py:44
  240.4 13.8 copy-start.4
  291.8 13.8 copy-start.4
  343.1 13.8 copy-start.4
  394.4 13.8 copy-start.4
  445.8 13.8 copy-start.4
  497.1 13.8 copy-start.4
  548.4 13.8 copy-start.4
  599.8 13.8 copy-start.4
  628.3 62.0 %copy-start.31 = (pred[8192]{0:T(1024)(128)(4,1)}, pred[8192]{0:T(1024)(128)(4,1)S(1)}, u32[]{:S(2)}) copy-start(pred[8192]{0:T(1024)(128)(4,1)S(1)} %get-tuple-element.862) | copy-start | bytes 24580
  628.3 62.0 %copy-start.35 = (s32[1024]{0:T(1024)}, s32[1024]{0:T(1024)S(1)}, u32[]{:S(2)}) copy-start(s32[1024]{0:T(1024)S(1)} %get-tuple-element.863) | copy-start | bytes 12292
  628.3 62.0 %copy-start.37 = (s32[1024]{0:T(1024)}, s32[1024]{0:T(1024)S(1)}, u32[]{:S(2)}) copy-start(s32[1024]{0:T(1024)S(1)} %get-tuple-element.864) | copy-start | bytes 12292
  629.3 61.0 %copy-start.25 = (s32[8192]{0:T(1024)S(1)}, s32[8192]{0:T(1024)}, u32[]{:S(2)}) copy-start(s32[8192]{0:T(1024)} %param.28) | copy-start | bytes 98308
  629.3 622.5 %all-gather.24.cloned.1.call-start = ((), (), s32[]{:S(2)}) async-start(), calls=%async_computation.13 | async-start | bytes 41943040 | tf_op jit(solution)/shard_map/all_gather | solution.py:40
  690.3 851.8 %reduce-scatter.7.cloned.1.call-start = ((), (), s32[]{:S(2)}) async-start(), calls=%async_computation.8 | async-start | bytes 41943040 | tf_op jit(solution)/shard_map/reduce_scatter | solution.py:69
  714.5 1948.4 %all-reduce.6.cloned.1.call-start = ((), (), s32[]{:S(2)}) async-start(), calls=%async_computation.17 | async-start | bytes 134217728
  1269.2 26.3 copy-start.29
  1295.4 3003.6 %copy-start.22 = (f32[4096]{0:T(1024)}, f32[4096]{0:T(1024)S(1)}, u32[]{:S(2)}) copy-start(f32[4096]{0:T(1024)S(1)} %add_rsqrt_fusion) | copy-start | bytes 49156
  1329.7 1505.9 %all-gather.18.cloned.1.call-start = ((), (), s32[]{:S(2)}) async-start(), calls=%async_computation.7 | async-start | bytes 20971520 | tf_op jit(solution)/shard_map/all_gather | solution.py:44
  2676.7 458.1 %all-gather.20.cloned.1.call-start = ((), (), s32[]{:S(2)}) async-start(), calls=%async_computation.9 | async-start | bytes 41943040 | tf_op jit(solution)/shard_map/all_gather | solution.py:73
  2684.6 1013.1 %all-gather.26.cloned.1.call-start = ((), (), s32[]{:S(2)}) async-start(), calls=%async_computation.14 | async-start | bytes 41943040 | tf_op jit(solution)/shard_map/all_gather | solution.py:40
  2850.8 1408.0 %all-gather.28.cloned.1.call-start = ((), (), s32[]{:S(2)}) async-start(), calls=%async_computation.15 | async-start | bytes 41943040 | tf_op jit(solution)/shard_map/all_gather | solution.py:40
  3161.9 1241.6 %reduce-scatter.9.cloned.1.call-start = ((), (), s32[]{:S(2)}) async-start(), calls=%async_computation.10 | async-start | bytes 10485760 | tf_op jit(solution)/shard_map/reduce_scatter | solution.py:69
  4275.6 23.5 copy-start.27
  4299.1 15.8 copy-start.15
  4320.5 87.2 %copy-start.5 = (bf16[8192,2,64]{0,2,1:T(8,128)(2,1)S(1)}, bf16[8192,2,64]{0,2,1:T(8,128)(2,1)}, u32[]{:S(2)}) copy-start(bf16[8192,2,64]{0,2,1:T(8,128)(2,1)} %get-tuple-element.812) | copy-start | bytes 6291460
  4320.5 87.2 %copy-start.19 = (s32[8192]{0:T(1024)S(1)}, s32[8192]{0:T(1024)}, u32[]{:S(2)}) copy-start(s32[8192]{0:T(1024)} %param.27) | copy-start | bytes 98308
  4320.5 87.2 %copy-start.32 = (pred[8192]{0:T(1024)(128)(4,1)S(1)}, pred[8192]{0:T(1024)(128)(4,1)}, u32[]{:S(2)}) copy-start(pred[8192]{0:T(1024)(128)(4,1)} %copy-done.31) | copy-start | bytes 24580
  4320.5 87.2 %copy-start.36 = (s32[1024]{0:T(1024)S(1)}, s32[1024]{0:T(1024)}, u32[]{:S(2)}) copy-start(s32[1024]{0:T(1024)} %copy-done.35) | copy-start | bytes 12292
  4320.5 87.2 %copy-start.38 = (s32[1024]{0:T(1024)S(1)}, s32[1024]{0:T(1024)}, u32[]{:S(2)}) copy-start(s32[1024]{0:T(1024)} %copy-done.37) | copy-start | bytes 12292
  4320.5 1003.3 %reduce-scatter.11.cloned.1.call-start = ((), (), s32[]{:S(2)}) async-start(), calls=%async_computation.11 | async-start | bytes 4718592 | tf_op jit(solution)/shard_map/reduce_scatter | solution.py:236
  4411.1 14.0 copy-start.6
  4481.3 12.0 copy-start.7
  4517.3 14.0 copy-start.6
  4587.4 12.0 copy-start.7
  4623.4 14.0 copy-start.6
  4693.6 12.0 copy-start.7
  4729.5 14.0 copy-start.6
  4799.7 12.0 copy-start.7
  4835.7 14.0 copy-start.6
  4905.9 12.0 copy-start.7
  4941.9 14.0 copy-start.6
  5012.1 12.0 copy-start.7
  5048.1 14.0 copy-start.6
  5118.2 12.0 copy-start.7
  5154.2 14.0 copy-start.6
  5224.4 12.0 copy-start.7
  5272.3 126.3 %all-gather.22.cloned.1.call-start = ((), (), s32[]{:S(2)}) async-start(), calls=%async_computation.12 | async-start | bytes 7864320 | tf_op jit(solution)/shard_map/all_gather | solution.py:73
  5274.2 54.2 copy-start.28
  5328.3 14.9 copy-start.23
  5328.3 14.9 copy-start.30
  5328.3 114.4 %all-reduce.8.cloned.1.call-start = ((), (), s32[]{:S(2)}) async-start(), calls=%async_computation.18 | async-start | bytes 15204352 | tf_op jit(solution)/shard_map/psum | solution.py:253
  5328.4 40.4 slice-start
  5343.3 25.6 slice-start.1
  5343.3 25.6 copy-start.12
  5368.8 29.8 copy-start.21
  5368.8 29.8 copy-start.33
  5372.0 35.8 copy-start.17
  5407.7 599.7 %all-gather.30.cloned.1.call-start = ((), (), s32[]{:S(2)}) async-start(), calls=%async_computation.16 | async-start | bytes 41943040 | tf_op jit(solution)/shard_map/all_gather | solution.py:40
  (21 other events, 140.1 us)
Sparse Core Ops, SparseCore 0:
  42.2 120.1 reduce-scatter.4
  168.3 36.6 all-gather.13
  629.4 52.6 all-gather.15
  690.4 561.3 all-gather.23
  1254.7 287.2 reduce-scatter.6
  1545.8 1116.9 all-reduce.5
  2676.8 158.8 all-gather.17
  2837.5 297.2 all-gather.19
  3136.3 561.3 all-gather.25
  3699.2 559.5 all-gather.27
  4320.7 82.7 reduce-scatter.8
  5272.5 51.2 reduce-scatter.10
  5328.4 70.1 all-gather.21
  5407.8 34.8 all-reduce.7
  5444.8 562.5 all-gather.29
